TPU v7x, 32 devices: a whole 2x2x4 slice. The times are simulated.
32 devices in a mesh: grp: 2 (over y), wide: 4 (over z), slc: 2 (over x), sub: 2 (over core).
Axes of the slice: x: 2, y: 2, z: 4, core: 2. Of those that a mesh axis runs over, the one named last changes fastest.
Arguments:
- a_stem: bfloat16 [2, 16, 2048, 256], P(None, ('grp', 'slc', 'sub'), 'wide'), parts along dimension 1, may hold values from -6 to 6
- b_stem: bfloat16 [2, 16, 256, 512], P(None, ('grp', 'slc', 'sub')), parts along dimension 1, may hold values from -0.09375 to 0.09375
- gate_pick: int32 [40], P('grp'), parts along dimension 0, may hold values from 0 to 2
- leg_order: int32 [18], P('grp'), parts along dimension 0, may hold values from 0 to 8, each once
Outputs:
- amplitudes: float32 [2, 8, 4, 4, 32, 512], P(None, 'grp', ('slc', 'sub'), 'wide'), parts along dimension 1
There are 2 independent parts, one for each index of `grp`. A program takes and returns all parts, laid end to end along the dimension named above; each array names one. Nothing has to cross between parts.
Inputs may be any that keep to these rules, and one draw needn't show every extreme that they name: `gate_pick`: an index into the three gates of the steps. `leg_order`: each column leg once.
All inputs are finite; a program needn't handle non-finite values.
Results may differ from a plain program's by a relative error of at most 0.0003.
Values sent between devices are 32-bit elements; how exact they have to be, the bound alone decides.
A program may use at most 320 MiB of HBM per device.

v0:
```python
import jax
import jax.numpy as jnp
from jax import lax
from jax.sharding import PartitionSpec as P

HALF_ROOT = 0.7071067811865476
GATE_REAL = (
    ((HALF_ROOT, 0.0), (0.0, HALF_ROOT)),
    ((HALF_ROOT, -HALF_ROOT), (HALF_ROOT, HALF_ROOT)),
    ((HALF_ROOT, -0.5), (0.5, HALF_ROOT)),
)
GATE_IMAG = (
    ((0.0, -HALF_ROOT), (-HALF_ROOT, 0.0)),
    ((0.0, 0.0), (0.0, 0.0)),
    ((0.0, -0.5), (-0.5, 0.0)),
)


def partner_2(value, axis, distance):
    mask = 2**distance
    pairs = [(source, source ^ mask) for source in range(lax.axis_size(axis))]
    return lax.ppermute(value, axis, pairs)


def gate_entries(picks):
    table_real = jnp.asarray(GATE_REAL, jnp.float32)
    table_imag = jnp.asarray(GATE_IMAG, jnp.float32)
    onehot = (picks[..., None] == jnp.arange(3, dtype=jnp.int32)).astype(jnp.float32)
    high = lax.Precision.HIGHEST
    u_real = jnp.tensordot(onehot, table_real, axes=1, precision=high)
    u_imag = jnp.tensordot(onehot, table_imag, axes=1, precision=high)
    return (u_real, u_imag)


def kron_matrix(picks):
    u_real, u_imag = gate_entries(picks)
    mat_real = jnp.ones((1, 1), jnp.float32)
    mat_imag = jnp.zeros((1, 1), jnp.float32)
    for position in range(picks.shape[0]):
        g_real = u_real[position]
        g_imag = u_imag[position]
        new_real = jnp.kron(mat_real, g_real) - jnp.kron(mat_imag, g_imag)
        new_imag = jnp.kron(mat_real, g_imag) + jnp.kron(mat_imag, g_real)
        mat_real, mat_imag = (new_real, new_imag)
    return (mat_real, mat_imag)


def complex_left(mat_real, mat_imag, field, columns):
    high = lax.Precision.HIGHEST
    first_term = jnp.dot(mat_real, field, precision=high, preferred_element_type=jnp.float32)
    second_term = jnp.dot(mat_imag, field, precision=high, preferred_element_type=jnp.float32)
    real_part = first_term[..., :columns] - second_term[..., columns:]
    imag_part = first_term[..., columns:] + second_term[..., :columns]
    return jnp.concatenate((real_part, imag_part), -1)


def pair_mix(field, partner, pick, mine, columns):
    u_real, u_imag = gate_entries(pick)
    self_real = jnp.where(mine == 0, u_real[0, 0], u_real[1, 1])
    self_imag = jnp.where(mine == 0, u_imag[0, 0], u_imag[1, 1])
    other_real = jnp.where(mine == 0, u_real[0, 1], u_real[1, 0])
    other_imag = jnp.where(mine == 0, u_imag[0, 1], u_imag[1, 0])
    own_real = field[..., :columns]
    own_imag = field[..., columns:]
    peer_real = partner[..., :columns]
    peer_imag = partner[..., columns:]
    real_part = (
        self_real * own_real
        - self_imag * own_imag
        + other_real * peer_real
        - other_imag * peer_imag
    )
    imag_part = (
        self_real * own_imag
        + self_imag * own_real
        + other_real * peer_imag
        + other_imag * peer_real
    )
    return jnp.concatenate((real_part, imag_part), -1)


def per_device(a_stem, b_stem, gate_pick, leg_order):
    columns = b_stem.shape[3]
    col_bits = columns.bit_length() - 1
    wide_count = lax.axis_size("wide")
    wide_bits = wide_count.bit_length() - 1
    group = lax.axis_size(("slc", "sub"))
    slice_bits = group.bit_length() - 1
    rows_dev = a_stem.shape[2]
    rows_loc = rows_dev // group
    loc_bits = rows_loc.bit_length() - 1
    row_bits = wide_bits + slice_bits + loc_bits
    high = lax.Precision.HIGHEST
    left_stem = jnp.concatenate((a_stem[0], a_stem[1]), axis=2)
    right_stem = jnp.concatenate(
        (jnp.concatenate((b_stem[0], b_stem[1]), 2), jnp.concatenate((-b_stem[1], b_stem[0]), 2)), 1
    )
    partial_value = jnp.einsum(
        "srk,skc->rc", left_stem, right_stem, preferred_element_type=jnp.float32
    )
    field = lax.psum_scatter(partial_value, ("slc", "sub"), scatter_dimension=0, tiled=True)
    group_index = lax.axis_index(("slc", "sub"))
    for bit_pos in range(slice_bits):
        partner = partner_2(field, ("slc", "sub"), bit_pos)
        mine = group_index >> bit_pos & 1
        field = pair_mix(
            field, partner, gate_pick[wide_bits + slice_bits - 1 - bit_pos], mine, columns
        )
    loc_real, loc_imag = kron_matrix(gate_pick[wide_bits + slice_bits : row_bits])
    field = complex_left(loc_real, loc_imag, field, columns)
    nat_real, nat_imag = kron_matrix(gate_pick[row_bits : row_bits + col_bits])
    positions = jnp.arange(columns, dtype=jnp.int32)
    source = jnp.zeros((columns,), jnp.int32)
    for out_bit in range(col_bits):
        source = source + ((positions >> out_bit & 1) << leg_order[out_bit])
    permute = (source[:, None] == positions[None, :]).astype(jnp.float32)
    col_real = jnp.dot(permute, nat_real, precision=high, preferred_element_type=jnp.float32)
    col_imag = jnp.dot(permute, nat_imag, precision=high, preferred_element_type=jnp.float32)
    combined = jnp.concatenate(
        (
            jnp.concatenate((col_real.T, col_imag.T), 1),
            jnp.concatenate((-col_imag.T, col_real.T), 1),
        ),
        0,
    )
    field = jnp.dot(field, combined, precision=high, preferred_element_type=jnp.float32)
    wide_index = lax.axis_index("wide")
    for bit_pos in range(wide_bits):
        partner = partner_2(field, "wide", bit_pos)
        mine = wide_index >> bit_pos & 1
        field = pair_mix(field, partner, gate_pick[wide_bits - 1 - bit_pos], mine, columns)
    split_rows = field.reshape(wide_count, rows_loc // wide_count, 2 * columns)
    placed = lax.all_to_all(split_rows, "wide", split_axis=0, concat_axis=0, tiled=True)
    stacked = jnp.stack((placed[..., :columns], placed[..., columns:]), 0)
    return stacked.reshape(2, wide_count, 1, 1, rows_loc // wide_count, columns)


def solution(mesh):
    placed = (
        P(None, ("grp", "slc", "sub"), "wide", None),
        P(None, ("grp", "slc", "sub"), None, None),
        P("grp"),
        P("grp"),
    )
    return jax.shard_map(
        per_device,
        mesh=mesh,
        in_specs=placed,
        out_specs=P(None, "grp", ("slc", "sub"), "wide", None, None),
        check_vma=False,
    )
```

profile of v0, /device:TPU:0, one launch (start us, length us, event | category | flops | bytes accessed | tf_op | source)
XLA Modules:
  0.0 330.8 jit_solution(15913786212140823650)
XLA Ops:
  6.5 1.3 slice_bitcast_fusion
  7.8 1.1 fusion.59
  8.9 1.3 slice_bitcast_fusion.3
  10.2 2.6 fusion.16
  16.3 4.1 %multiply_subtract_fusion.2 = (f32[64,2,64,2]{3,2,1,0:T(8,128)}, f32[64,2,64,2]{3,2,1,0:T(8,128)}) fusion(f32[2,2]{1,0:T(2,128)S(1)} %get-tuple-element.137, f32[64,64]{1,0:T(8,128)S(1)} %add.291, f32[2,2]{1,0:T(2,128)S(1)} %get-tuple-element.21, f32[64,64]{1,0:T(8,128)S(1)} %sub.201), kind=kLoop, calls=%fused_computation.13 | loop fusion | flops 98304 | bytes 163872 | tf_op jit(solution)/shard_map/sub | solution.py:42
  20.4 4.1 %add.293 = f32[128,128]{1,0:T(8,128)S(1)} reshape(f32[64,2,64,2]{3,2,1,0:T(8,128)} %get-tuple-element.60) | data formatting | bytes 131072 | tf_op jit(solution)/shard_map/add | solution.py:43
  24.6 4.1 %sub.203 = f32[128,128]{1,0:T(8,128)S(1)} reshape(f32[64,2,64,2]{3,2,1,0:T(8,128)} %get-tuple-element.59) | data formatting | bytes 131072 | tf_op jit(solution)/shard_map/sub | solution.py:42
  28.7 11.6 %multiply_subtract_fusion.1 = (f32[128,2,128,2]{3,2,1,0:T(8,128)}, f32[128,2,128,2]{3,2,1,0:T(8,128)}) fusion(f32[2,2]{1,0:T(2,128)S(1)} %get-tuple-element.138, f32[128,128]{1,0:T(8,128)S(1)} %add.293, f32[2,2]{1,0:T(2,128)S(1)} %get-tuple-element.20, f32[128,128]{1,0:T(8,128)S(1)} %sub.203), kind=kLoop, calls=%fused_computation.3 | loop fusion | flops 393216 | bytes 655392 | tf_op jit(solution)/shard_map/sub | solution.py:42
  40.3 12.7 %add.295 = f32[256,256]{1,0:T(8,128)S(1)} reshape(f32[128,2,128,2]{3,2,1,0:T(8,128)} %get-tuple-element.56) | data formatting | bytes 524288 | tf_op jit(solution)/shard_map/add | solution.py:43
  53.0 12.7 %sub.205 = f32[256,256]{1,0:T(8,128)S(1)} reshape(f32[128,2,128,2]{3,2,1,0:T(8,128)} %get-tuple-element.55) | data formatting | bytes 524288 | tf_op jit(solution)/shard_map/sub | solution.py:42
  65.7 41.5 %multiply_add_fusion = (f32[256,2,256,2]{3,2,1,0:T(8,128)}, f32[256,2,256,2]{3,2,1,0:T(8,128)}) fusion(f32[2,2]{1,0:T(2,128)S(1)} %get-tuple-element.139, f32[256,256]{1,0:T(8,128)S(1)} %add.295, f32[2,2]{1,0:T(2,128)S(1)} %get-tuple-element.19, f32[256,256]{1,0:T(8,128)S(1)} %sub.205), kind=kLoop, calls=%fused_computation | loop fusion | flops 1572864 | bytes 2621472 | tf_op jit(solution)/shard_map/add | solution.py:43
  107.3 47.0 %sub.207 = f32[512,512]{1,0:T(8,128)S(1)} reshape(f32[256,2,256,2]{3,2,1,0:T(8,128)} %get-tuple-element.52) | data formatting | bytes 2097152 | tf_op jit(solution)/shard_map/sub | solution.py:42
  154.4 47.0 %add.305 = f32[512,512]{1,0:T(8,128)S(1)} reshape(f32[256,2,256,2]{3,2,1,0:T(8,128)} %get-tuple-element.51) | data formatting | bytes 2097152 | tf_op jit(solution)/shard_map/add | solution.py:43
  203.1 1.4 multiply_subtract_fusion.5
  204.5 1.8 add.268
  207.0 4.2 %multiply_subtract_fusion.3 = (f32[64,2,64,2]{3,2,1,0:T(8,128)}, f32[64,2,64,2]{3,2,1,0:T(8,128)}) fusion(f32[2,2]{1,0:T(2,128)S(1)} %get-tuple-element.146, f32[64,64]{1,0:T(8,128)S(1)} %add.268, f32[2,2]{1,0:T(2,128)S(1)} %get-tuple-element.5, f32[64,64]{1,0:T(8,128)S(1)} %sub.183), kind=kLoop, calls=%fused_computation.15 | loop fusion | flops 98304 | bytes 163872 | tf_op jit(solution)/shard_map/sub | solution.py:42
  211.2 4.0 %add.279 = f32[128,128]{1,0:T(8,128)S(1)} reshape(f32[64,2,64,2]{3,2,1,0:T(8,128)} %get-tuple-element.58) | data formatting | bytes 131072 | tf_op jit(solution)/shard_map/add | solution.py:43
  215.2 4.0 %sub.185 = f32[128,128]{1,0:T(8,128)S(1)} reshape(f32[64,2,64,2]{3,2,1,0:T(8,128)} %get-tuple-element.57) | data formatting | bytes 131072 | tf_op jit(solution)/shard_map/sub | solution.py:42
  219.8 0.7 fusion.39
  220.6 0.7 fusion.67
  222.5 0.7 fusion.40
  223.2 0.7 fusion.66
  227.7 0.8 fusion.41
  228.4 0.7 fusion.65
  230.9 0.8 fusion.42
  231.7 0.7 fusion.64
  236.1 0.7 fusion.69
  236.7 5.6 %shift-left_add_fusion = s32[512]{0:T(512)S(1)} fusion(s32[]{:T(128)} %bitcast.59, s32[]{:T(128)} %bitcast.58, s32[]{:T(128)} %bitcast.57, s32[]{:T(128)} %bitcast.56, s32[]{:T(128)} %bitcast.55, s32[]{:T(128)} %bitcast.54, s32[]{:T(128)} %bitcast.53, s32[]{:T(128)} %bitcast.52, s32[]{:T(128)} %bitcast.51), kind=kLoop, calls=%fused_computation.111 | loop fusion | flops 17920 | bytes 2084 | tf_op jit(solution)/shard_map/add | solution.py:115
  242.4 1.2 multiply_add_fusion.10
  243.6 2.7 collective-permute-start.1
  246.3 1.1 fusion.23
  247.4 1.1 fusion.70
  248.5 10.3 %collective-permute-done.1 = f32[128,1024]{1,0:T(8,128)S(1)} collective-permute-done((f32[128,1024]{1,0:T(8,128)S(1)}, f32[128,1024]{1,0:T(8,128)S(1)}, u32[]{:S(2)}, u32[]{:S(2)}) %collective-permute-start.1) | collective-permute-done | bytes 524320 | tf_op jit(solution)/shard_map/ppermute | solution.py:22
  260.2 4.5 %fusion = f32[128,1024]{1,0:T(8,128)S(1)} fusion(f32[512,512]{0,1:T(8,128)S(1)} %fusion.23, f32[512,512]{0,1:T(8,128)S(1)} %get-tuple-element.130, f32[512,512]{0,1:T(8,128)S(1)} %get-tuple-element.131, f32[128,512]{1,0:T(8,128)S(1)} %get-tuple-element.42, f32[128,512]{1,0:T(8,128)S(1)} %get-tuple-element.41), kind=kOutput, calls=%fused_computation.4 | convolution fusion | flops 1613889536 | bytes 4194304 | tf_op jit(solution)/shard_map/dot_general | solution.py:126
  264.7 1.9 collective-permute-start.2
  266.6 0.7 fusion.43
  267.3 0.7 fusion.63
  269.2 0.7 fusion.44
  269.9 0.7 fusion.62
  274.3 4.3 %collective-permute-done.2 = f32[128,1024]{1,0:T(8,128)S(1)} collective-permute-done((f32[128,1024]{1,0:T(8,128)S(1)}, f32[128,1024]{1,0:T(8,128)S(1)}, u32[]{:S(2)}, u32[]{:S(2)}) %collective-permute-start.2) | collective-permute-done | bytes 524320 | tf_op jit(solution)/shard_map/ppermute | solution.py:22
  278.7 2.7 collective-permute-start.3
  281.4 0.8 fusion.45
  282.3 0.7 fusion.61
  284.3 0.8 fusion.46
  285.1 0.7 fusion.60
  289.6 14.2 %collective-permute-done.3 = f32[128,1024]{1,0:T(8,128)S(1)} collective-permute-done((f32[128,1024]{1,0:T(8,128)S(1)}, f32[128,1024]{1,0:T(8,128)S(1)}, u32[]{:S(2)}, u32[]{:S(2)}) %collective-permute-start.3) | collective-permute-done | bytes 524320 | tf_op jit(solution)/shard_map/ppermute | solution.py:22
  304.0 19.1 %all_to_all.5 = f32[4,32,1024]{2,1,0:T(8,128)S(1)} all-to-all(f32[4,32,1024]{2,1,0:T(8,128)S(1)} %bitcast.168), channel_id=1, replica_groups=mesh['grp'=2,'wide'=4,'slc'=2,'sub'=2] {'wide'}, dimensions={0} | all-to-all | bytes 1048576 | tf_op jit(solution)/shard_map/all_to_all | solution.py:133
  323.1 0.8 maximum_bitcast_fusion
  (70 shorter events, 8.8 us)
Async XLA Ops:
  6.5 223.9 %reduce-scatter.2.cloned.1.call-start = ((), (), s32[]{:S(2)}) async-start(), calls=%async_computation.2 | async-start | bytes 2621440 | tf_op jit(solution)/shard_map/reduce_scatter | solution.py:101
  10.2 2.7 copy-start.3
  10.2 2.7 copy-start.1
  10.2 2.9 copy-start.2
  211.1 8.7 %copy-start.5 = (f32[3,2,2]{0,2,1:T(2,128)S(1)}, f32[3,2,2]{0,2,1:T(2,128)}, u32[]{:S(2)}) copy-start(f32[3,2,2]{0,2,1:T(2,128)} %constant.42.clone) | copy-start | bytes 148
  211.2 11.3 %copy-start.4 = (f32[3,2,2]{0,2,1:T(2,128)S(1)}, f32[3,2,2]{0,2,1:T(2,128)}, u32[]{:S(2)}) copy-start(f32[3,2,2]{0,2,1:T(2,128)} %constant.41.clone) | copy-start | bytes 148
  211.2 24.9 %copy-start = (s32[9]{0:T(128)S(1)}, s32[9]{0:T(128)}, u32[]{:S(2)}) copy-start(s32[9]{0:T(128)} %param.19) | copy-start | bytes 112
  230.4 12.0 %collective-permute-start = (f32[128,1024]{1,0:T(8,128)}, f32[128,1024]{1,0:T(8,128)S(1)}, u32[]{:S(2)}, u32[]{:S(2)}) collective-permute-start(f32[128,1024]{1,0:T(8,128)} %reduce-scatter.2.cloned.1.call-done), channel_id=1, source_target_pairs={{0,1},{1,0},{2,3},{3,2},{4,5},{5,4},{6,7},{7,6},{8,9},{9,8},{10,11... | collective-permute-start | bytes 1572872 | tf_op jit(solution)/shard_map/ppermute | solution.py:22
  243.6 15.2 %collective-permute-start.1 = (f32[128,1024]{1,0:T(8,128)S(1)}, f32[128,1024]{1,0:T(8,128)S(1)}, u32[]{:S(2)}, u32[]{:S(2)}) collective-permute-start(f32[128,1024]{1,0:T(8,128)S(1)} %pad_maximum_fusion), channel_id=1, source_target_pairs={{0,2},{1,3},{2,0},{3,1},{4,6},{5,7},{6,4},{7,5},{8,10},{9,11},{10,... | collective-permute-start | bytes 1572872 | tf_op jit(solution)/shard_map/ppermute | solution.py:22
  264.7 13.8 %collective-permute-start.2 = (f32[128,1024]{1,0:T(8,128)S(1)}, f32[128,1024]{1,0:T(8,128)S(1)}, u32[]{:S(2)}, u32[]{:S(2)}) collective-permute-start(f32[128,1024]{1,0:T(8,128)S(1)} %fusion), channel_id=1, source_target_pairs={{0,4},{4,0},{8,12},{12,8},{1,5},{5,1},{9,13},{13,9},{2,6},{6,2},{1... | collective-permute-start | bytes 1572872 | tf_op jit(solution)/shard_map/ppermute | solution.py:22
  278.7 25.1 %collective-permute-start.3 = (f32[128,1024]{1,0:T(8,128)S(1)}, f32[128,1024]{1,0:T(8,128)S(1)}, u32[]{:S(2)}, u32[]{:S(2)}) collective-permute-start(f32[128,1024]{1,0:T(8,128)S(1)} %pad_maximum_fusion.2), channel_id=1, source_target_pairs={{0,8},{4,12},{8,0},{12,4},{1,9},{5,13},{9,1},{13,5},{2,10},{6,14},... | collective-permute-start | bytes 1572872 | tf_op jit(solution)/shard_map/ppermute | solution.py:22
Sparse Core Ops, SparseCore 0:
  13.0 34.1 reduce-scatter.1
where the time goes:
time: 333 us; the launch traced here: 331 us
  local copies, waits for them, and re-layouts  151 us (45%)
  other arithmetic  73.3 us (22%)
  between operations  33.6 us (10%)
  waiting for transfers between devices  28.8 us (9%)
  blocking collectives  19.1 us (6%)
  matrix products  16.9 us (5%)
  starting transfers between devices  7.8 us (2%)
    add x14, local copies, waits for them, and re-layouts, kron_matrix(): new_imag = jnp.kron(mat_real, g_imag) + jnp.kron(mat_imag, g_real)  71.2 us
    sub x14, local copies, waits for them, and re-layouts, kron_matrix(): new_real = jnp.kron(mat_real, g_real) - jnp.kron(mat_imag, g_imag)  69.9 us
    add x1, other arithmetic, kron_matrix(): new_imag = jnp.kron(mat_real, g_imag) + jnp.kron(mat_imag, g_real)  41.5 us
    ppermute x4, waiting for transfers between devices, partner_2(): return lax.ppermute(value, axis, pairs)  28.8 us
    sub x15, other arithmetic, kron_matrix(): new_real = jnp.kron(mat_real, g_real) - jnp.kron(mat_imag, g_imag)  22.5 us
    all_to_all x1, blocking collectives, per_device(): lax.all_to_all(split_rows, 'wide', split_axis=0, concat_axis=0, tiled=True)  19.1 us
    ppermute x4, starting transfers between devices, partner_2(): return lax.ppermute(value, axis, pairs)  7.8 us
  transfers between devices with their start and end apart: 5, of which 3 were waited for; matrix products, arithmetic and copies ran while one was open for 69% of the time, Pallas kernels for 0%

commit v1 on v0

v1 whole, which is shorter than its diff:
```python
import functools

import jax
import jax.numpy as jnp
from jax import lax
from jax.experimental import pallas as pl
from jax.experimental.pallas import tpu as pltpu
from jax.sharding import PartitionSpec as P

HALF_ROOT = 0.7071067811865476
MESH = pl.DeviceIdType.MESH


def eighth_turns(pick):
    return jnp.where(pick == 0, 2, jnp.where(pick == 2, 1, 0)).astype(jnp.int32)


def bit_of(value, position):
    return lax.shift_right_logical(value, jnp.full_like(value, position)) & 1


def turn_cos(turns):
    angle = turns & 7
    size = jnp.where((angle & 1) == 1, HALF_ROOT, jnp.where((angle & 2) == 0, 1.0, 0.0))
    return jnp.where(((angle + 2) & 4) == 4, -size, size).astype(jnp.float32)


def turn_sin(turns):
    return turn_cos(turns + 6)


def sign_of(target, source):
    value = (~target) & source
    for step in (8, 4, 2, 1):
        value = value ^ lax.shift_right_logical(value, jnp.full_like(value, step))
    return (1 - 2 * (value & 1)).astype(jnp.float32)


def butterfly(blocks):
    count = len(blocks)
    mask = 1
    while mask < count:
        mixed = list(blocks)
        for index in range(count):
            if not index & mask:
                low, high = blocks[index], blocks[index | mask]
                mixed[index] = low - high
                mixed[index | mask] = low + high
        blocks = mixed
        mask *= 2
    return blocks


def split_two(value):
    top = value.astype(jnp.bfloat16)
    rest = (value - top.astype(jnp.float32)).astype(jnp.bfloat16)
    return top, rest


def kernel_body(
    dims,
    pick_ref, order_ref, a_hbm, b_hbm, out_ref,
    a_vm, b_vm, row_cos, row_sin, row_mat, col_mat, out_cos, out_sin,
    sub_out, sub_in, slc_out, slc_in, wide_out, wide_in, acc,
    a_sem, b_sem, sub_ss, sub_rs, slc_ss, slc_rs, wide_ss, wide_rs,
):
    (n_sub, n_slc, n_wide, slices, rows_loc, loc, loc_pad, columns, width) = dims
    f32 = jnp.float32
    i32 = jnp.int32
    group = n_sub * n_slc
    chunks = columns // width
    col_bits = columns.bit_length() - 1
    wide_bits = n_wide.bit_length() - 1
    group_bits = group.bit_length() - 1
    rows_bits = rows_loc.bit_length() - 1
    loc_bits = loc.bit_length() - 1
    row_bits = wide_bits + group_bits + rows_bits
    me_sub = lax.axis_index("sub")
    me_slc = lax.axis_index("slc")
    me_wide = lax.axis_index("wide")
    me_group = me_slc * n_sub + me_sub

    a_copy = pltpu.make_async_copy(a_hbm, a_vm, a_sem)
    b_copies = [
        pltpu.make_async_copy(
            b_hbm.at[:, :, :, pl.ds(c * width, width)], b_vm.at[c], b_sem.at[c]
        )
        for c in range(chunks)
    ]
    b_copies[0].start()
    a_copy.start()
    for c in range(1, chunks):
        b_copies[c].start()

    barrier = pltpu.get_barrier_semaphore()
    for axis, me, count in (("sub", me_sub, n_sub), ("slc", me_slc, n_slc), ("wide", me_wide, n_wide)):
        for k in range(1, count):
            pl.semaphore_signal(
                barrier, inc=1, device_id={axis: lax.rem(me + k, count)}, device_id_type=MESH
            )

    turns = [eighth_turns(pick_ref[q]) for q in range(row_bits + col_bits)]

    def scalar_turns(value, first, count):
        total = jnp.int32(0)
        for j in range(count):
            total = total + turns[first + count - 1 - j] * (lax.shift_right_logical(value, jnp.int32(j)) & 1)
        return total

    def vector_turns(value, first, count):
        total = jnp.zeros_like(value)
        for j in range(count):
            total = total + turns[first + count - 1 - j] * bit_of(value, j)
        return total

    row_iota = lax.broadcasted_iota(i32, (rows_loc, 128), 0)
    row_turns = vector_turns(row_iota, wide_bits + group_bits, rows_bits)
    row_turns = row_turns + scalar_turns(me_wide.astype(i32), 0, wide_bits)
    for s in range(group):
        here = row_turns + scalar_turns(jnp.int32(s), wide_bits, group_bits)
        row_cos[s] = turn_cos(here)
        row_sin[s] = turn_sin(here)

    def stem(c):
        b_copies[c].wait()
        rights = []
        for j in range(slices):
            b_real = b_vm[c, 0, j]
            b_imag = b_vm[c, 1, j]
            rights.append(jnp.concatenate((b_real, b_imag), 1))
            rights.append(jnp.concatenate((-b_imag, b_real), 1))
        reals, imags = [], []
        for s in range(group):
            total = None
            for j in range(slices):
                for part in range(2):
                    term = jnp.dot(
                        a_vm[part, j, pl.ds(s * rows_loc, rows_loc), :],
                        rights[2 * j + part],
                        preferred_element_type=f32,
                    )
                    total = term if total is None else total + term
            real, imag = total[:, :width], total[:, width:]
            cos, sin = row_cos[s], row_sin[s]
            reals.append(real * cos - imag * sin)
            imags.append(real * sin + imag * cos)
        reals = butterfly(reals)
        imags = butterfly(imags)
        for s in range(group):
            slc, sub = s // n_sub, s % n_sub
            sub_out[c, sub, slc, :, :width] = reals[s]
            sub_out[c, sub, slc, :, width:] = imags[s]

    def sub_copies(c):
        copies = []
        for k in range(1, n_sub):
            peer = lax.rem(me_sub + k, n_sub)
            copies.append(
                pltpu.make_async_remote_copy(
                    src_ref=sub_out.at[c, peer], dst_ref=sub_in.at[c, k - 1],
                    send_sem=sub_ss.at[c, k - 1], recv_sem=sub_rs.at[c, k - 1],
                    device_id={"sub": peer}, device_id_type=MESH,
                )
            )
        return copies

    def slc_copies(c):
        copies = []
        for k in range(1, n_slc):
            peer = lax.rem(me_slc + k, n_slc)
            copies.append(
                pltpu.make_async_remote_copy(
                    src_ref=slc_out.at[c, k - 1], dst_ref=slc_in.at[c, k - 1],
                    send_sem=slc_ss.at[c, k - 1], recv_sem=slc_rs.at[c, k - 1],
                    device_id={"slc": peer}, device_id_type=MESH,
                )
            )
        return copies

    def wide_copies(c):
        copies = []
        for k in range(1, n_wide):
            peer = lax.rem(me_wide + k, n_wide)
            copies.append(
                pltpu.make_async_remote_copy(
                    src_ref=wide_out.at[c, peer, pl.ds(0, loc)],
                    dst_ref=wide_in.at[c, k - 1, pl.ds(0, loc)],
                    send_sem=wide_ss.at[c, k - 1], recv_sem=wide_rs.at[c, k - 1],
                    device_id={"wide": peer}, device_id_type=MESH,
                )
            )
        return copies

    all_sub = [sub_copies(c) for c in range(chunks)]
    all_slc = [slc_copies(c) for c in range(chunks)]
    all_wide = [wide_copies(c) for c in range(chunks)]

    def to_slc(c):
        for copy in all_sub[c]:
            copy.wait_recv()
        for k in range(1, n_slc):
            peer = lax.rem(me_slc + k, n_slc)
            total = sub_out[c, me_sub, peer]
            for j in range(n_sub - 1):
                total = total + sub_in[c, j, peer]
            slc_out[c, k - 1] = total
            all_slc[c][k - 1].start()

    col_turns = vector_turns(lax.broadcasted_iota(i32, (1, columns), 1), row_bits, col_bits)
    col_cos = turn_cos(col_turns)
    col_sin = turn_sin(col_turns)

    def to_wide(c):
        total = sub_out[c, me_sub, me_slc]
        for j in range(n_sub - 1):
            total = total + sub_in[c, j, me_slc]
        for k in range(1, n_slc):
            all_slc[c][k - 1].wait_recv()
            total = total + slc_in[c, k - 1]
        real, imag = total[:, :width], total[:, width:]
        cos = col_cos[:, c * width:(c + 1) * width]
        sin = col_sin[:, c * width:(c + 1) * width]
        turned = jnp.concatenate((real * cos - imag * sin, real * sin + imag * cos), 1)
        top, rest = split_two(turned)
        mat = row_mat[...]
        mixed = jnp.dot(mat, top, preferred_element_type=f32) + jnp.dot(
            mat, rest, preferred_element_type=f32
        )
        for h in range(n_wide):
            wide_out[c, h] = mixed[h * loc_pad:(h + 1) * loc_pad]
        for copy in all_wide[c]:
            copy.start()

    def finish(c):
        for copy in all_wide[c]:
            copy.wait_recv()
        wide_in[c, n_wide - 1] = wide_out[c, me_wide]
        blocks = []
        for w in range(n_wide):
            slot = lax.rem(me_wide - w - 1 + 2 * n_wide, n_wide)
            blocks.append(wide_in[c, slot])
        blocks = butterfly(blocks)
        stacked = jnp.concatenate(
            [b[:, :width] for b in blocks] + [b[:, width:] for b in blocks], 0
        )
        top, rest = split_two(stacked)
        mat = col_mat[pl.ds(c * width, width), :]
        term = jnp.dot(top, mat, preferred_element_type=f32) + jnp.dot(
            rest, mat, preferred_element_type=f32
        )
        if c == 0:
            acc[...] = term
        elif c < chunks - 1:
            acc[...] += term
        else:
            total = acc[...] + term
            half = n_wide * loc_pad
            real, imag = total[:half], total[half:]
            cos, sin = out_cos[...], out_sin[...]
            out_real = real * cos + imag * sin
            out_imag = imag * cos - real * sin
            for w in range(n_wide):
                out_ref[0, w] = out_real[w * loc_pad:w * loc_pad + loc]
                out_ref[1, w] = out_imag[w * loc_pad:w * loc_pad + loc]

    a_copy.wait()
    stem(0)
    pl.semaphore_wait(barrier, (n_sub - 1) + (n_slc - 1) + (n_wide - 1))
    for copy in all_sub[0]:
        copy.start()
    for c in range(1, chunks):
        stem(c)
        for copy in all_sub[c]:
            copy.start()
        to_slc(c - 1)
    to_slc(chunks - 1)

    shape = (n_wide * loc_pad, rows_loc)
    spot = lax.broadcasted_iota(i32, shape, 0)
    low = spot & (loc_pad - 1)
    high = lax.shift_right_logical(spot, jnp.full_like(spot, loc_pad.bit_length() - 1))
    entry = sign_of(high * loc + low, lax.broadcasted_iota(i32, shape, 1))
    row_mat[...] = jnp.where(low < loc, entry, 0.0).astype(jnp.bfloat16)

    positions = lax.broadcasted_iota(i32, (1, columns), 1)
    source = jnp.zeros((1, columns), i32)
    for j in range(col_bits):
        source = source + bit_of(positions, j) * lax.shift_left(jnp.int32(1), order_ref[j])
    for c in range(chunks):
        inner = lax.broadcasted_iota(i32, (width, columns), 0) + c * width
        col_mat[pl.ds(c * width, width), :] = sign_of(
            jnp.broadcast_to(source, (width, columns)), inner
        ).astype(jnp.bfloat16)

    legs = row_bits + col_bits
    scale = 0.5 ** (legs // 2) * (HALF_ROOT if legs % 2 else 1.0)
    place = lax.broadcasted_iota(i32, (n_wide * loc_pad, 1), 0)
    inner_loc = place & (loc_pad - 1)
    outer = lax.shift_right_logical(place, jnp.full_like(place, loc_pad.bit_length() - 1))
    end_turns = vector_turns(outer, 0, wide_bits)
    end_turns = end_turns + vector_turns(inner_loc, row_bits - loc_bits, loc_bits)
    end_turns = end_turns + scalar_turns(me_group.astype(i32), wide_bits, group_bits)
    end_turns = end_turns + scalar_turns(me_wide.astype(i32), wide_bits + group_bits, rows_bits - loc_bits)
    end_turns = end_turns + vector_turns(source, row_bits, col_bits)
    out_cos[...] = turn_cos(end_turns) * scale
    out_sin[...] = turn_sin(end_turns) * scale

    to_wide(0)
    for c in range(1, chunks):
        to_wide(c)
        finish(c - 1)
    finish(chunks - 1)
    for copies in all_sub + all_slc + all_wide:
        for copy in copies:
            copy.wait_send()


def per_device(a_stem, b_stem, gate_pick, leg_order):
    columns = b_stem.shape[3]
    slices = a_stem.shape[1]
    bond = a_stem.shape[3]
    n_wide = lax.axis_size("wide")
    n_slc = lax.axis_size("slc")
    n_sub = lax.axis_size("sub")
    group = n_slc * n_sub
    rows_dev = a_stem.shape[2]
    rows_loc = rows_dev // group
    loc = rows_loc // n_wide
    loc_pad = max(loc, 8)
    width = 128
    chunks = columns // width
    dims = (n_sub, n_slc, n_wide, slices, rows_loc, loc, loc_pad, columns, width)
    f32, bf16 = jnp.float32, jnp.bfloat16
    tall = n_wide * loc_pad
    dma = pltpu.SemaphoreType.DMA
    out = pl.pallas_call(
        functools.partial(kernel_body, dims),
        out_shape=jax.ShapeDtypeStruct((2, n_wide, loc, columns), f32),
        in_specs=[
            pl.BlockSpec(memory_space=pltpu.SMEM),
            pl.BlockSpec(memory_space=pltpu.SMEM),
            pl.BlockSpec(memory_space=pl.ANY),
            pl.BlockSpec(memory_space=pl.ANY),
        ],
        out_specs=pl.BlockSpec(memory_space=pltpu.VMEM),
        scratch_shapes=[
            pltpu.VMEM((2, slices, rows_dev, bond), bf16),
            pltpu.VMEM((chunks, 2, slices, bond, width), bf16),
            pltpu.VMEM((group, rows_loc, 128), f32),
            pltpu.VMEM((group, rows_loc, 128), f32),
            pltpu.VMEM((tall, rows_loc), bf16),
            pltpu.VMEM((columns, columns), bf16),
            pltpu.VMEM((tall, columns), f32),
            pltpu.VMEM((tall, columns), f32),
            pltpu.VMEM((chunks, n_sub, n_slc, rows_loc, 2 * width), f32),
            pltpu.VMEM((chunks, n_sub - 1, n_slc, rows_loc, 2 * width), f32),
            pltpu.VMEM((chunks, n_slc - 1, rows_loc, 2 * width), f32),
            pltpu.VMEM((chunks, n_slc - 1, rows_loc, 2 * width), f32),
            pltpu.VMEM((chunks, n_wide, loc_pad, 2 * width), f32),
            pltpu.VMEM((chunks, n_wide, loc_pad, 2 * width), f32),
            pltpu.VMEM((2 * tall, columns), f32),
            dma,
            dma((chunks,)),
            dma((chunks, n_sub - 1)),
            dma((chunks, n_sub - 1)),
            dma((chunks, n_slc - 1)),
            dma((chunks, n_slc - 1)),
            dma((chunks, n_wide - 1)),
            dma((chunks, n_wide - 1)),
        ],
        compiler_params=pltpu.CompilerParams(
            collective_id=0, has_side_effects=True, vmem_limit_bytes=48 * 2**20
        ),
    )(gate_pick, leg_order, a_stem, b_stem)
    return out.reshape(2, n_wide, 1, 1, loc, columns)


def solution(mesh):
    placed = (
        P(None, ("grp", "slc", "sub"), "wide", None),
        P(None, ("grp", "slc", "sub"), None, None),
        P("grp"),
        P("grp"),
    )
    return jax.shard_map(
        per_device,
        mesh=mesh,
        in_specs=placed,
        out_specs=P(None, "grp", ("slc", "sub"), "wide", None, None),
        check_vma=False,
    )
```

time: 333 us -> 30.7 us (0.09)
  local copies, waits for them, and re-layouts: 151 us -> 4.55 us
  other arithmetic: 73.3 us -> 0 us
  between operations: 33.6 us -> 0.01 us
  waiting for transfers between devices: 28.8 us -> 0 us
  Pallas kernels: 0 us -> 26 us
  blocking collectives: 19.1 us -> 0 us
  matrix products: 16.9 us -> 0 us
  starting transfers between devices: 7.8 us -> 0 us
    add x14 -> x0, local copies, waits for them, and re-layouts: 71.2 us -> none  [kron_matrix(): new_imag = jnp.kron(mat_real, g_imag) + jnp.kron(mat_imag, g_real)]
    sub x14 -> x0, local copies, waits for them, and re-layouts: 69.9 us -> none  [kron_matrix(): new_real = jnp.kron(mat_real, g_real) - jnp.kron(mat_imag, g_imag)]
    add x4 -> x0, other arithmetic: 48.5 us -> none  [the longest x1 41.5 us: kron_matrix(): new_imag = jnp.kron(mat_real, g_imag) + jnp.kron(mat_imag, g_real)]
    ppermute x4 -> x0, waiting for transfers between devices: 28.8 us -> none  [partner_2(): return lax.ppermute(value, axis, pairs)]
    pallas_call x0 -> x1, Pallas kernels: none -> 26 us  [per_device(): pl.pallas_call(functools.partial(kernel_body, dims), out_shape=jax.ShapeD...]
    sub x18 -> x0, other arithmetic: 22.8 us -> none  [the longest x15 22.5 us: kron_matrix(): new_real = jnp.kron(mat_real, g_real) - jnp.kron(mat_imag, g_imag)]
    all_to_all x1 -> x0, blocking collectives: 19.1 us -> none  [per_device(): lax.all_to_all(split_rows, 'wide', split_axis=0, concat_axis=0, tiled=True)]
    dot_general x14 -> x0, matrix products: 16.4 us -> none  [the longest x1 4.46 us: per_device(): jnp.dot(field, combined, precision=high, preferred_element_type=jnp.float32)]
  transfers between devices with their start and end apart: 5 -> 0, of which waited for: 3 -> 0; matrix products, arithmetic and copies ran while one was open for 69% -> 0% of each run, Pallas kernels for 0% -> 0%
where the time goes in v1:
time: 30.7 us; the launch traced here: 30.5 us
  Pallas kernels  26 us (85%)
  local copies, waits for them, and re-layouts  4.55 us (15%)
    pallas_call x1, Pallas kernels, per_device(): pl.pallas_call(functools.partial(kernel_body, dims), out_shape=jax.ShapeD...  26 us
    unnamed x9, local copies, waits for them, and re-layouts  4.55 us

profile of v1, /device:TPU:0, one launch (start us, length us, event | category | flops | bytes accessed | tf_op | source)
XLA Modules:
  0.0 30.5 jit_solution(18236906204811181033)
XLA Ops:
  0.0 0.0 copy-start
  0.0 1.2 %copy-done = bf16[2,2,512,256]{3,2,1,0:T(8,128)(2,1)S(1)} copy-done((bf16[2,2,512,256]{3,2,1,0:T(8,128)(2,1)S(1)}, bf16[2,2,512,256]{3,2,1,0:T(8,128)(2,1)}, u32[]{:S(2)}) %copy-start) | copy-done | bytes 1048600
  1.2 0.0 copy-start.1
  1.2 1.2 %copy-done.1 = bf16[2,2,256,512]{3,2,1,0:T(8,128)(2,1)S(1)} copy-done((bf16[2,2,256,512]{3,2,1,0:T(8,128)(2,1)S(1)}, bf16[2,2,256,512]{3,2,1,0:T(8,128)(2,1)}, u32[]{:S(2)}) %copy-start.1) | copy-done | bytes 1048600
  2.5 0.0 copy-start.2
  2.5 0.7 %copy-done.2 = s32[20]{0:T(128)S(1)} copy-done((s32[20]{0:T(128)S(1)}, s32[20]{0:T(128)}, u32[]{:S(2)}) %copy-start.2) | copy-done | bytes 104
  3.1 0.0 copy-start.3
  3.1 0.7 %copy-done.3 = s32[9]{0:T(128)S(1)} copy-done((s32[9]{0:T(128)S(1)}, s32[9]{0:T(128)}, u32[]{:S(2)}) %copy-start.3) | copy-done | bytes 60
  3.8 26.0 %shard_map.46 = f32[2,4,32,512]{3,2,1,0:T(8,128)S(1)} custom-call(s32[20]{0:T(128)S(1)} %copy-done.2, s32[9]{0:T(128)S(1)} %copy-done.3, bf16[2,2,512,256]{3,2,1,0:T(8,128)(2,1)S(1)} %copy-done, bf16[2,2,256,512]{3,2,1,0:T(8,128)(2,1)S(1)} %copy-done.1), custom_call_target="tpu_custom_call" | custom-call | tf_op jit(solution)/shard_map/pallas_call | solution.py:336
  29.7 0.8 %copy.7 = f32[2,4,1,1,32,512]{5,4,3,2,1,0:T(8,128)} copy(f32[2,4,1,1,32,512]{5,4,3,2,1,0:T(8,128)S(1)} %bitcast.3) | data formatting | bytes 1048576
Async XLA Ops:
  0.0 1.2 %copy-start = (bf16[2,2,512,256]{3,2,1,0:T(8,128)(2,1)S(1)}, bf16[2,2,512,256]{3,2,1,0:T(8,128)(2,1)}, u32[]{:S(2)}) copy-start(bf16[2,2,512,256]{3,2,1,0:T(8,128)(2,1)} %a_hbm.1) | copy-start | bytes 3145732
  1.2 1.2 %copy-start.1 = (bf16[2,2,256,512]{3,2,1,0:T(8,128)(2,1)S(1)}, bf16[2,2,256,512]{3,2,1,0:T(8,128)(2,1)}, u32[]{:S(2)}) copy-start(bf16[2,2,256,512]{3,2,1,0:T(8,128)(2,1)} %b_hbm.1) | copy-start | bytes 3145732
  2.5 0.7 %copy-start.2 = (s32[20]{0:T(128)S(1)}, s32[20]{0:T(128)}, u32[]{:S(2)}) copy-start(s32[20]{0:T(128)} %pick_ref.1) | copy-start | bytes 244
  3.1 0.7 %copy-start.3 = (s32[9]{0:T(128)S(1)}, s32[9]{0:T(128)}, u32[]{:S(2)}) copy-start(s32[9]{0:T(128)} %order_ref.1) | copy-start | bytes 112

commit v2 on v1

v2 whole, which is shorter than its diff:
```python
import functools

import jax
import jax.numpy as jnp
from jax import lax
from jax.experimental import pallas as pl
from jax.experimental.pallas import tpu as pltpu
from jax.sharding import PartitionSpec as P

HALF_ROOT = 0.7071067811865476
MESH = pl.DeviceIdType.MESH


def eighth_turns(pick):
    return jnp.where(pick == 0, 2, jnp.where(pick == 2, 1, 0)).astype(jnp.int32)


def bit_of(value, position):
    return lax.shift_right_logical(value, jnp.full_like(value, position)) & 1


def turn_cos(turns):
    angle = turns & 7
    size = jnp.where((angle & 1) == 1, HALF_ROOT, jnp.where((angle & 2) == 0, 1.0, 0.0))
    return jnp.where(((angle + 2) & 4) == 4, -size, size).astype(jnp.float32)


def turn_sin(turns):
    return turn_cos(turns + 6)


def sign_of(target, source):
    value = (~target) & source
    for step in (8, 4, 2, 1):
        value = value ^ lax.shift_right_logical(value, jnp.full_like(value, step))
    return (1 - 2 * (value & 1)).astype(jnp.float32)


def butterfly(blocks):
    count = len(blocks)
    mask = 1
    while mask < count:
        mixed = list(blocks)
        for index in range(count):
            if not index & mask:
                low, high = blocks[index], blocks[index | mask]
                mixed[index] = low - high
                mixed[index | mask] = low + high
        blocks = mixed
        mask *= 2
    return blocks


def split_two(value):
    top = value.astype(jnp.bfloat16)
    rest = (value - top.astype(jnp.float32)).astype(jnp.bfloat16)
    return top, rest


def kernel_body(
    dims,
    pick_hbm, order_hbm, a_hbm, b_hbm, out_ref,
    pick_ref, order_ref, a_vm, b_vm, row_cos, row_sin, row_mat, col_mat, out_cos, out_sin,
    sub_out, sub_in, slc_out, slc_in, wide_out, wide_in, acc,
    pick_sem, order_sem, a_sem, b_sem, sub_ss, sub_rs, slc_ss, slc_rs, wide_ss, wide_rs,
    lower_in, upper_in,
):
    (n_sub, n_slc, n_wide, slices, rows_loc, loc, loc_pad, columns, width) = dims
    f32 = jnp.float32
    i32 = jnp.int32
    group = n_sub * n_slc
    chunks = columns // width
    col_bits = columns.bit_length() - 1
    wide_bits = n_wide.bit_length() - 1
    group_bits = group.bit_length() - 1
    rows_bits = rows_loc.bit_length() - 1
    loc_bits = loc.bit_length() - 1
    row_bits = wide_bits + group_bits + rows_bits
    me_sub = lax.axis_index("sub")
    me_slc = lax.axis_index("slc")
    me_wide = lax.axis_index("wide")
    me_group = me_slc * n_sub + me_sub

    barrier = pltpu.get_barrier_semaphore()
    for axis, me, count in (("sub", me_sub, n_sub), ("slc", me_slc, n_slc)):
        for k in range(1, count):
            pl.semaphore_signal(
                barrier, inc=1, device_id={axis: lax.rem(me + k, count)}, device_id_type=MESH
            )

    @pl.when(me_wide > 0)
    def _():
        pl.semaphore_signal(barrier, inc=1, device_id={"wide": me_wide - 1}, device_id_type=MESH)

    @pl.when(me_wide < n_wide - 1)
    def _():
        pl.semaphore_signal(barrier, inc=1, device_id={"wide": me_wide + 1}, device_id_type=MESH)

    pick_copy = pltpu.make_async_copy(pick_hbm, pick_ref, pick_sem)
    order_copy = pltpu.make_async_copy(order_hbm, order_ref, order_sem)
    a_copy = pltpu.make_async_copy(a_hbm, a_vm, a_sem)
    b_copies = [
        pltpu.make_async_copy(
            b_hbm.at[:, :, :, pl.ds(c * width, width)], b_vm.at[c], b_sem.at[c]
        )
        for c in range(chunks)
    ]
    pick_copy.start()
    order_copy.start()
    b_copies[0].start()
    a_copy.start()
    for c in range(1, chunks):
        b_copies[c].start()

    shape = (n_wide * loc_pad, rows_loc)
    spot = lax.broadcasted_iota(i32, shape, 0)
    low = spot & (loc_pad - 1)
    high = lax.shift_right_logical(spot, jnp.full_like(spot, loc_pad.bit_length() - 1))
    entry = sign_of(high * loc + low, lax.broadcasted_iota(i32, shape, 1))
    row_mat[...] = jnp.where(low < loc, entry, 0.0).astype(jnp.bfloat16)

    pick_copy.wait()
    order_copy.wait()
    turns = [eighth_turns(pick_ref[q]) for q in range(row_bits + col_bits)]

    def scalar_turns(value, first, count):
        total = jnp.int32(0)
        for j in range(count):
            total = total + turns[first + count - 1 - j] * (lax.shift_right_logical(value, jnp.int32(j)) & 1)
        return total

    def vector_turns(value, first, count):
        total = jnp.zeros_like(value)
        for j in range(count):
            total = total + turns[first + count - 1 - j] * bit_of(value, j)
        return total

    row_iota = lax.broadcasted_iota(i32, (rows_loc, 128), 0)
    row_turns = vector_turns(row_iota, wide_bits + group_bits, rows_bits)
    row_turns = row_turns + scalar_turns(me_wide.astype(i32), 0, wide_bits)
    for s in range(group):
        here = row_turns + scalar_turns(jnp.int32(s), wide_bits, group_bits)
        row_cos[s] = turn_cos(here)
        row_sin[s] = turn_sin(here)
    col_turns = vector_turns(lax.broadcasted_iota(i32, (1, columns), 1), row_bits, col_bits)
    col_cos = turn_cos(col_turns)
    col_sin = turn_sin(col_turns)

    def stem(c):
        b_copies[c].wait()
        rights = []
        for j in range(slices):
            b_real = b_vm[c, 0, j]
            b_imag = b_vm[c, 1, j]
            rights.append(jnp.concatenate((b_real, b_imag), 1))
            rights.append(jnp.concatenate((-b_imag, b_real), 1))
        right = jnp.concatenate(rights, 0)
        ccos = col_cos[:, c * width:(c + 1) * width]
        csin = col_sin[:, c * width:(c + 1) * width]
        reals, imags = [], []
        for s in range(group):
            left = jnp.concatenate(
                [
                    a_vm[part, j, pl.ds(s * rows_loc, rows_loc), :]
                    for j in range(slices)
                    for part in range(2)
                ],
                1,
            )
            total = jnp.dot(left, right, preferred_element_type=f32)
            real, imag = total[:, :width], total[:, width:]
            cos, sin = row_cos[s], row_sin[s]
            real, imag = real * cos - imag * sin, real * sin + imag * cos
            reals.append(real * ccos - imag * csin)
            imags.append(real * csin + imag * ccos)
        reals = butterfly(reals)
        imags = butterfly(imags)
        mat = row_mat[...]
        for s in range(group):
            slc, sub = s // n_sub, s % n_sub
            top, rest = split_two(jnp.concatenate((reals[s], imags[s]), 1))
            mixed = jnp.dot(mat, top, preferred_element_type=f32) + jnp.dot(
                mat, rest, preferred_element_type=f32
            )
            for h in range(n_wide):
                sub_out[c, sub, slc, h] = mixed[h * loc_pad:(h + 1) * loc_pad]

    def place_of(i):
        left = jnp.where(i < n_wide - 1 - me_wide, n_wide - 1 - i, i - (n_wide - 1 - me_wide))
        right = jnp.where(i < me_wide, i, n_wide - 1 - (i - me_wide))
        return jnp.where(me_wide < n_wide // 2, left, right)

    places = [place_of(i) for i in range(n_wide - 1)] + [me_wide]

    all_sub = []
    for c in range(chunks):
        for k in range(1, n_sub):
            peer = lax.rem(me_sub + k, n_sub)
            all_sub.append(
                pltpu.make_async_remote_copy(
                    src_ref=sub_out.at[c, peer], dst_ref=sub_in.at[c, k - 1],
                    send_sem=sub_ss.at[c, k - 1], recv_sem=sub_rs.at[c, k - 1],
                    device_id={"sub": peer}, device_id_type=MESH,
                )
            )

    def slc_copy(i, c, k):
        return pltpu.make_async_remote_copy(
            src_ref=slc_out.at[i, c, k - 1], dst_ref=slc_in.at[i, c, k - 1],
            send_sem=slc_ss.at[i, c, k - 1], recv_sem=slc_rs.at[i, c, k - 1],
            device_id={"slc": lax.rem(me_slc + k, n_slc)}, device_id_type=MESH,
        )

    all_slc = {
        (i, c, k): slc_copy(i, c, k)
        for i in range(n_wide) for c in range(chunks) for k in range(1, n_slc)
    }

    def wide_copy(i, c, owner):
        return pltpu.make_async_remote_copy(
            src_ref=wide_out.at[i, c, pl.ds(0, loc)],
            dst_ref=wide_in.at[owner, c, pl.ds(0, loc)],
            send_sem=wide_ss.at[i, c], recv_sem=wide_rs.at[owner, c],
            device_id={"wide": places[i]}, device_id_type=MESH,
        )

    all_wide = {
        (i, c): wide_copy(i, c, me_wide) for i in range(n_wide - 1) for c in range(chunks)
    }

    def send_sub(c):
        for k in range(n_sub - 1):
            all_sub[c * (n_sub - 1) + k].start()

    def to_slc(i, c):
        if i == 0:
            for k in range(n_sub - 1):
                all_sub[c * (n_sub - 1) + k].wait_recv()
        for k in range(1, n_slc):
            peer = lax.rem(me_slc + k, n_slc)
            total = sub_out[c, me_sub, peer, places[i]]
            for j in range(n_sub - 1):
                total = total + sub_in[c, j, peer, places[i]]
            slc_out[i, c, k - 1] = total
            all_slc[i, c, k].start()

    def summed(i, c):
        total = sub_out[c, me_sub, me_slc, places[i]]
        for j in range(n_sub - 1):
            total = total + sub_in[c, j, me_slc, places[i]]
        for k in range(1, n_slc):
            all_slc[i, c, k].wait_recv()
            total = total + slc_in[i, c, k - 1]
        return total

    def to_wide(i, c):
        wide_out[i, c] = summed(i, c)
        all_wide[i, c].start()

    def finish(i):
        pieces = []
        for c in range(chunks):
            if i < n_wide - 1:
                wide_copy(i, c, places[i]).wait_recv()
                pieces.append(wide_in[places[i], c])
            else:
                pieces.append(summed(i, c))
        stacked = jnp.concatenate(
            (
                jnp.concatenate([piece[:, :width] for piece in pieces], 1),
                jnp.concatenate([piece[:, width:] for piece in pieces], 1),
            ),
            0,
        )
        top, rest = split_two(stacked)
        both = jnp.dot(
            jnp.concatenate((top, rest), 0), col_mat[...], preferred_element_type=f32
        )
        acc[places[i]] = both[:2 * loc_pad] + both[2 * loc_pad:]

    a_copy.wait()
    ahead = min(3, chunks)
    for c in range(ahead):
        stem(c)
    ends = jnp.where(me_wide == 0, 1, 0) + jnp.where(me_wide == n_wide - 1, 1, 0)
    pl.semaphore_wait(barrier, (n_sub - 1) + (n_slc - 1) + 2 - ends)
    for c in range(ahead):
        send_sub(c)

    def tell(token, target):
        pl.semaphore_signal(token, inc=1, device_id={"wide": target}, device_id_type=MESH)

    if n_wide > 2:
        @pl.when(me_wide == n_wide - 2)
        def _():
            tell(upper_in, me_wide - 1)

        @pl.when(me_wide == 1)
        def _():
            tell(lower_in, me_wide + 1)

    for c in range(ahead, chunks):
        stem(c)
        send_sub(c)
    for c in range(chunks):
        to_slc(0, c)

    if n_wide > 2:
        @pl.when(me_wide <= n_wide - 3)
        def _():
            pl.semaphore_wait(upper_in, 1)

            @pl.when(me_wide >= 1)
            def _():
                tell(upper_in, me_wide - 1)

        @pl.when(me_wide >= 2)
        def _():
            pl.semaphore_wait(lower_in, 1)

            @pl.when(me_wide <= n_wide - 2)
            def _():
                tell(lower_in, me_wide + 1)

    for i in range(1, n_wide):
        for c in range(chunks):
            to_slc(i, c)

    positions = lax.broadcasted_iota(i32, (1, columns), 1)
    source = jnp.zeros((1, columns), i32)
    for j in range(col_bits):
        source = source + bit_of(positions, j) * lax.shift_left(jnp.int32(1), order_ref[j])

    def build_columns(c):
        inner = lax.broadcasted_iota(i32, (width, columns), 0) + c * width
        col_mat[pl.ds(c * width, width), :] = sign_of(
            jnp.broadcast_to(source, (width, columns)), inner
        ).astype(jnp.bfloat16)

    def build_exit():
        legs = row_bits + col_bits
        scale = 0.5 ** (legs // 2) * (HALF_ROOT if legs % 2 else 1.0)
        place = lax.broadcasted_iota(i32, (n_wide * loc_pad, 1), 0)
        inner_loc = place & (loc_pad - 1)
        outer = lax.shift_right_logical(place, jnp.full_like(place, loc_pad.bit_length() - 1))
        end = vector_turns(outer, 0, wide_bits)
        end = end + vector_turns(inner_loc, row_bits - loc_bits, loc_bits)
        end = end + scalar_turns(me_group.astype(i32), wide_bits, group_bits)
        end = end + scalar_turns(me_wide.astype(i32), wide_bits + group_bits, rows_bits - loc_bits)
        end = end + vector_turns(source, row_bits, col_bits)
        out_cos[...] = turn_cos(end) * scale
        out_sin[...] = turn_sin(end) * scale

    for c in range(chunks):
        build_columns(c)
    for i in range(n_wide - 1):
        for c in range(chunks):
            to_wide(i, c)
    build_exit()
    for i in range(n_wide - 2):
        finish(i)
    finish(n_wide - 1)
    finish(n_wide - 2)
    blocks = butterfly([acc[w] for w in range(n_wide)])
    for w in range(n_wide):
        real, imag = blocks[w][:loc], blocks[w][loc_pad:loc_pad + loc]
        cos = out_cos[w * loc_pad:w * loc_pad + loc]
        sin = out_sin[w * loc_pad:w * loc_pad + loc]
        out_ref[0, w] = real * cos + imag * sin
        out_ref[1, w] = imag * cos - real * sin
    for copy in all_sub + list(all_slc.values()) + list(all_wide.values()):
        copy.wait_send()


def per_device(a_stem, b_stem, gate_pick, leg_order):
    columns = b_stem.shape[3]
    slices = a_stem.shape[1]
    bond = a_stem.shape[3]
    n_wide = lax.axis_size("wide")
    n_slc = lax.axis_size("slc")
    n_sub = lax.axis_size("sub")
    group = n_slc * n_sub
    rows_dev = a_stem.shape[2]
    rows_loc = rows_dev // group
    loc = rows_loc // n_wide
    loc_pad = max(loc, 8)
    width = 128
    chunks = columns // width
    dims = (n_sub, n_slc, n_wide, slices, rows_loc, loc, loc_pad, columns, width)
    f32, bf16 = jnp.float32, jnp.bfloat16
    tall = n_wide * loc_pad
    dma = pltpu.SemaphoreType.DMA
    block = (loc_pad, 2 * width)
    out = pl.pallas_call(
        functools.partial(kernel_body, dims),
        out_shape=jax.ShapeDtypeStruct((2, n_wide, loc, columns), f32),
        in_specs=[pl.BlockSpec(memory_space=pltpu.HBM)] * 4,
        out_specs=pl.BlockSpec(memory_space=pltpu.VMEM),
        scratch_shapes=[
            pltpu.SMEM(gate_pick.shape, jnp.int32),
            pltpu.SMEM(leg_order.shape, jnp.int32),
            pltpu.VMEM((2, slices, rows_dev, bond), bf16),
            pltpu.VMEM((chunks, 2, slices, bond, width), bf16),
            pltpu.VMEM((group, rows_loc, 128), f32),
            pltpu.VMEM((group, rows_loc, 128), f32),
            pltpu.VMEM((tall, rows_loc), bf16),
            pltpu.VMEM((columns, columns), bf16),
            pltpu.VMEM((tall, columns), f32),
            pltpu.VMEM((tall, columns), f32),
            pltpu.VMEM((chunks, n_sub, n_slc, n_wide) + block, f32),
            pltpu.VMEM((chunks, n_sub - 1, n_slc, n_wide) + block, f32),
            pltpu.VMEM((n_wide, chunks, n_slc - 1) + block, f32),
            pltpu.VMEM((n_wide, chunks, n_slc - 1) + block, f32),
            pltpu.VMEM((n_wide, chunks) + block, f32),
            pltpu.VMEM((n_wide, chunks) + block, f32),
            pltpu.VMEM((n_wide, 2 * loc_pad, columns), f32),
            dma,
            dma,
            dma,
            dma((chunks,)),
            dma((chunks, n_sub - 1)),
            dma((chunks, n_sub - 1)),
            dma((n_wide, chunks, n_slc - 1)),
            dma((n_wide, chunks, n_slc - 1)),
            dma((n_wide, chunks)),
            dma((n_wide, chunks)),
            pltpu.SemaphoreType.REGULAR,
            pltpu.SemaphoreType.REGULAR,
        ],
        compiler_params=pltpu.CompilerParams(
            collective_id=0, has_side_effects=True, vmem_limit_bytes=48 * 2**20
        ),
    )(gate_pick, leg_order, a_stem, b_stem)
    return out.reshape(2, n_wide, 1, 1, loc, columns)


def solution(mesh):
    placed = (
        P(None, ("grp", "slc", "sub"), "wide", None),
        P(None, ("grp", "slc", "sub"), None, None),
        P("grp"),
        P("grp"),
    )
    return jax.shard_map(
        per_device,
        mesh=mesh,
        in_specs=placed,
        out_specs=P(None, "grp", ("slc", "sub"), "wide", None, None),
        check_vma=False,
    )
```

time: 30.7 us -> 28.4 us (0.925)
  Pallas kernels: 26 us -> 23.5 us
    pallas_call x1, Pallas kernels: 26 us -> 23.5 us  [per_device(): pl.pallas_call(functools.partial(kernel_body, dims), out_shape=jax.ShapeD...]
where the time goes in v2:
time: 28.4 us; the launch traced here: 28 us
  Pallas kernels  23.5 us (83%)
  local copies, waits for them, and re-layouts  4.55 us (16%)
    pallas_call x1, Pallas kernels, per_device(): pl.pallas_call(functools.partial(kernel_body, dims), out_shape=jax.ShapeD...  23.5 us
    unnamed x9, local copies, waits for them, and re-layouts  4.55 us

profile of v2, /device:TPU:0, one launch (start us, length us, event | category | flops | bytes accessed | tf_op | source)
XLA Modules:
  0.0 28.0 jit_solution(5919550818582765124)
XLA Ops:
  0.0 0.0 copy-start
  0.0 1.2 %copy-done = bf16[2,2,512,256]{3,2,1,0:T(8,128)(2,1)S(1)} copy-done((bf16[2,2,512,256]{3,2,1,0:T(8,128)(2,1)S(1)}, bf16[2,2,512,256]{3,2,1,0:T(8,128)(2,1)}, u32[]{:S(2)}) %copy-start) | copy-done | bytes 1048600
  1.2 0.0 copy-start.1
  1.2 1.2 %copy-done.1 = bf16[2,2,256,512]{3,2,1,0:T(8,128)(2,1)S(1)} copy-done((bf16[2,2,256,512]{3,2,1,0:T(8,128)(2,1)S(1)}, bf16[2,2,256,512]{3,2,1,0:T(8,128)(2,1)}, u32[]{:S(2)}) %copy-start.1) | copy-done | bytes 1048600
  2.5 0.0 copy-start.2
  2.5 0.7 %copy-done.2 = s32[20]{0:T(128)S(1)} copy-done((s32[20]{0:T(128)S(1)}, s32[20]{0:T(128)}, u32[]{:S(2)}) %copy-start.2) | copy-done | bytes 104
  3.1 0.0 copy-start.3
  3.1 0.7 %copy-done.3 = s32[9]{0:T(128)S(1)} copy-done((s32[9]{0:T(128)S(1)}, s32[9]{0:T(128)}, u32[]{:S(2)}) %copy-start.3) | copy-done | bytes 60
  3.8 23.5 %shard_map.46 = f32[2,4,32,512]{3,2,1,0:T(8,128)S(1)} custom-call(s32[20]{0:T(128)S(1)} %copy-done.2, s32[9]{0:T(128)S(1)} %copy-done.3, bf16[2,2,512,256]{3,2,1,0:T(8,128)(2,1)S(1)} %copy-done, bf16[2,2,256,512]{3,2,1,0:T(8,128)(2,1)S(1)} %copy-done.1), custom_call_target="tpu_custom_call" | custom-call | tf_op jit(solution)/shard_map/pallas_call | solution.py:394
  27.2 0.8 %copy.7 = f32[2,4,1,1,32,512]{5,4,3,2,1,0:T(8,128)} copy(f32[2,4,1,1,32,512]{5,4,3,2,1,0:T(8,128)S(1)} %bitcast.3) | data formatting | bytes 1048576
Async XLA Ops:
  0.0 1.2 %copy-start = (bf16[2,2,512,256]{3,2,1,0:T(8,128)(2,1)S(1)}, bf16[2,2,512,256]{3,2,1,0:T(8,128)(2,1)}, u32[]{:S(2)}) copy-start(bf16[2,2,512,256]{3,2,1,0:T(8,128)(2,1)} %a_hbm.1) | copy-start | bytes 3145732
  1.2 1.2 %copy-start.1 = (bf16[2,2,256,512]{3,2,1,0:T(8,128)(2,1)S(1)}, bf16[2,2,256,512]{3,2,1,0:T(8,128)(2,1)}, u32[]{:S(2)}) copy-start(bf16[2,2,256,512]{3,2,1,0:T(8,128)(2,1)} %b_hbm.1) | copy-start | bytes 3145732
  2.5 0.7 %copy-start.2 = (s32[20]{0:T(128)S(1)}, s32[20]{0:T(128)}, u32[]{:S(2)}) copy-start(s32[20]{0:T(128)} %pick_hbm.1) | copy-start | bytes 244
  3.1 0.7 %copy-start.3 = (s32[9]{0:T(128)S(1)}, s32[9]{0:T(128)}, u32[]{:S(2)}) copy-start(s32[9]{0:T(128)} %order_hbm.1) | copy-start | bytes 112

commit v3 on v2

--- a/solution.py
+++ b/solution.py
@@ -59,10 +59,10 @@
 
 def kernel_body(
     dims,
-    pick_hbm, order_hbm, a_hbm, b_hbm, out_ref,
-    pick_ref, order_ref, a_vm, b_vm, row_cos, row_sin, row_mat, col_mat, out_cos, out_sin,
+    pick_hbm, a_hbm, b_hbm, out_ref,
+    pick_ref, a_vm, b_vm, row_cos, row_sin, row_mat, col_mat, out_cos, out_sin,
     sub_out, sub_in, slc_out, slc_in, wide_out, wide_in, acc,
-    pick_sem, order_sem, a_sem, b_sem, sub_ss, sub_rs, slc_ss, slc_rs, wide_ss, wide_rs,
+    pick_sem, a_sem, b_sem, sub_ss, sub_rs, slc_ss, slc_rs, wide_ss, wide_rs,
     lower_in, upper_in,
 ):
     (n_sub, n_slc, n_wide, slices, rows_loc, loc, loc_pad, columns, width) = dims
@@ -97,7 +97,6 @@
         pl.semaphore_signal(barrier, inc=1, device_id={"wide": me_wide + 1}, device_id_type=MESH)
 
     pick_copy = pltpu.make_async_copy(pick_hbm, pick_ref, pick_sem)
-    order_copy = pltpu.make_async_copy(order_hbm, order_ref, order_sem)
     a_copy = pltpu.make_async_copy(a_hbm, a_vm, a_sem)
     b_copies = [
         pltpu.make_async_copy(
@@ -106,7 +105,6 @@
         for c in range(chunks)
     ]
     pick_copy.start()
-    order_copy.start()
     b_copies[0].start()
     a_copy.start()
     for c in range(1, chunks):
@@ -120,7 +118,6 @@
     row_mat[...] = jnp.where(low < loc, entry, 0.0).astype(jnp.bfloat16)
 
     pick_copy.wait()
-    order_copy.wait()
     turns = [eighth_turns(pick_ref[q]) for q in range(row_bits + col_bits)]
 
     def scalar_turns(value, first, count):
@@ -279,7 +276,7 @@
         acc[places[i]] = both[:2 * loc_pad] + both[2 * loc_pad:]
 
     a_copy.wait()
-    ahead = min(3, chunks)
+    ahead = min(1, chunks)
     for c in range(ahead):
         stem(c)
     ends = jnp.where(me_wide == 0, 1, 0) + jnp.where(me_wide == n_wide - 1, 1, 0)
@@ -329,7 +326,7 @@
     positions = lax.broadcasted_iota(i32, (1, columns), 1)
     source = jnp.zeros((1, columns), i32)
     for j in range(col_bits):
-        source = source + bit_of(positions, j) * lax.shift_left(jnp.int32(1), order_ref[j])
+        source = source + bit_of(positions, j) * lax.shift_left(jnp.int32(1), pick_ref[row_bits + col_bits + j])
 
     def build_columns(c):
         inner = lax.broadcasted_iota(i32, (width, columns), 0) + c * width
@@ -391,14 +388,14 @@
     tall = n_wide * loc_pad
     dma = pltpu.SemaphoreType.DMA
     block = (loc_pad, 2 * width)
+    choices = jnp.concatenate((gate_pick, leg_order))
     out = pl.pallas_call(
         functools.partial(kernel_body, dims),
         out_shape=jax.ShapeDtypeStruct((2, n_wide, loc, columns), f32),
-        in_specs=[pl.BlockSpec(memory_space=pltpu.HBM)] * 4,
+        in_specs=[pl.BlockSpec(memory_space=pltpu.HBM)] * 3,
         out_specs=pl.BlockSpec(memory_space=pltpu.VMEM),
         scratch_shapes=[
-            pltpu.SMEM(gate_pick.shape, jnp.int32),
-            pltpu.SMEM(leg_order.shape, jnp.int32),
+            pltpu.SMEM(choices.shape, jnp.int32),
             pltpu.VMEM((2, slices, rows_dev, bond), bf16),
             pltpu.VMEM((chunks, 2, slices, bond, width), bf16),
             pltpu.VMEM((group, rows_loc, 128), f32),
@@ -416,7 +413,6 @@
             pltpu.VMEM((n_wide, 2 * loc_pad, columns), f32),
             dma,
             dma,
-            dma,
             dma((chunks,)),
             dma((chunks, n_sub - 1)),
             dma((chunks, n_sub - 1)),
@@ -428,9 +424,9 @@
             pltpu.SemaphoreType.REGULAR,
         ],
         compiler_params=pltpu.CompilerParams(
-            collective_id=0, has_side_effects=True, vmem_limit_bytes=48 * 2**20
+            collective_id=0, has_side_effects=True, vmem_limit_bytes=53 * 2**20
         ),
-    )(gate_pick, leg_order, a_stem, b_stem)
+    )(choices, a_stem, b_stem)
     return out.reshape(2, n_wide, 1, 1, loc, columns)
 
 

time: 28.4 us -> 25 us (0.88)
  local copies, waits for them, and re-layouts: 4.55 us -> 0.8 us
  other arithmetic: 0 us -> 0.75 us
    unnamed x9 -> x1, local copies, waits for them, and re-layouts: 4.55 us -> 0.8 us
    concatenate x0 -> x1, other arithmetic: none -> 0.75 us  [per_device(): choices = jnp.concatenate((gate_pick, leg_order))]
where the time goes in v3:
time: 25 us; the launch traced here: 24.8 us
  Pallas kernels  23.3 us (93%)
  local copies, waits for them, and re-layouts  0.8 us (3%)
  other arithmetic  0.75 us (3%)
    pallas_call x1, Pallas kernels, per_device(): pl.pallas_call(functools.partial(kernel_body, dims), out_shape=jax.ShapeD...  23.3 us
    unnamed x1, local copies, waits for them, and re-layouts  0.8 us
    concatenate x1, other arithmetic, per_device(): choices = jnp.concatenate((gate_pick, leg_order))  0.75 us

profile of v3, /device:TPU:0, one launch (start us, length us, event | category | flops | bytes accessed | tf_op | source)
XLA Modules:
  0.0 24.8 jit_solution(441819936749743234)
XLA Ops:
  0.0 0.7 %pad_add_fusion.pick_hbm = s32[29]{0:T(128)S(1)} fusion(s32[9]{0:T(128)} %param.7, s32[20]{0:T(128)} %param.6), kind=kLoop, calls=%fused_computation | loop fusion | flops 29 | bytes 232 | tf_op jit(solution)/shard_map/concatenate | solution.py:391
  0.7 23.3 %shard_map.46 = f32[2,4,32,512]{3,2,1,0:T(8,128)S(1)} custom-call(s32[29]{0:T(128)S(1)} %pad_add_fusion.pick_hbm, bf16[2,2,512,256]{3,2,1,0:T(8,128)(2,1)} %a_hbm.1, bf16[2,2,256,512]{3,2,1,0:T(8,128)(2,1)} %b_hbm.1), custom_call_target="tpu_custom_call" | custom-call | tf_op jit(solution)/shard_map/pallas_call | solution.py:392
  24.0 0.8 %copy.7 = f32[2,4,1,1,32,512]{5,4,3,2,1,0:T(8,128)} copy(f32[2,4,1,1,32,512]{5,4,3,2,1,0:T(8,128)S(1)} %bitcast.3) | data formatting | bytes 1048576

commit v4 on v3

--- a/solution.py
+++ b/solution.py
@@ -115,7 +115,8 @@
     low = spot & (loc_pad - 1)
     high = lax.shift_right_logical(spot, jnp.full_like(spot, loc_pad.bit_length() - 1))
     entry = sign_of(high * loc + low, lax.broadcasted_iota(i32, shape, 1))
-    row_mat[...] = jnp.where(low < loc, entry, 0.0).astype(jnp.bfloat16)
+    entry = jnp.where(low < loc, entry, 0.0).astype(jnp.bfloat16)
+    row_mat[...] = jnp.concatenate((entry, entry), 1)
 
     pick_copy.wait()
     turns = [eighth_turns(pick_ref[q]) for q in range(row_bits + col_bits)]
@@ -176,8 +177,8 @@
         for s in range(group):
             slc, sub = s // n_sub, s % n_sub
             top, rest = split_two(jnp.concatenate((reals[s], imags[s]), 1))
-            mixed = jnp.dot(mat, top, preferred_element_type=f32) + jnp.dot(
-                mat, rest, preferred_element_type=f32
+            mixed = jnp.dot(
+                mat, jnp.concatenate((top, rest), 0), preferred_element_type=f32
             )
             for h in range(n_wide):
                 sub_out[c, sub, slc, h] = mixed[h * loc_pad:(h + 1) * loc_pad]
@@ -189,17 +190,19 @@
 
     places = [place_of(i) for i in range(n_wide - 1)] + [me_wide]
 
-    all_sub = []
-    for c in range(chunks):
-        for k in range(1, n_sub):
-            peer = lax.rem(me_sub + k, n_sub)
-            all_sub.append(
-                pltpu.make_async_remote_copy(
-                    src_ref=sub_out.at[c, peer], dst_ref=sub_in.at[c, k - 1],
-                    send_sem=sub_ss.at[c, k - 1], recv_sem=sub_rs.at[c, k - 1],
-                    device_id={"sub": peer}, device_id_type=MESH,
-                )
-            )
+    def sub_copy(c, k, turn):
+        peer = lax.rem(me_sub + k, n_sub)
+        row = lax.rem(me_slc + turn, n_slc)
+        return pltpu.make_async_remote_copy(
+            src_ref=sub_out.at[c, peer, row], dst_ref=sub_in.at[c, k - 1, row],
+            send_sem=sub_ss.at[c, k - 1, turn], recv_sem=sub_rs.at[c, k - 1, turn],
+            device_id={"sub": peer}, device_id_type=MESH,
+        )
+
+    all_sub = {
+        (c, k, turn): sub_copy(c, k, turn)
+        for c in range(chunks) for k in range(1, n_sub) for turn in range(n_slc)
+    }
 
     def slc_copy(i, c, k):
         return pltpu.make_async_remote_copy(
@@ -226,14 +229,15 @@
     }
 
     def send_sub(c):
-        for k in range(n_sub - 1):
-            all_sub[c * (n_sub - 1) + k].start()
+        for turn in list(range(1, n_slc)) + [0]:
+            for k in range(1, n_sub):
+                all_sub[c, k, turn].start()
 
     def to_slc(i, c):
-        if i == 0:
-            for k in range(n_sub - 1):
-                all_sub[c * (n_sub - 1) + k].wait_recv()
         for k in range(1, n_slc):
+            if i == 0:
+                for j in range(1, n_sub):
+                    all_sub[c, j, k].wait_recv()
             peer = lax.rem(me_slc + k, n_slc)
             total = sub_out[c, me_sub, peer, places[i]]
             for j in range(n_sub - 1):
@@ -242,6 +246,9 @@
             all_slc[i, c, k].start()
 
     def summed(i, c):
+        if i == 0:
+            for k in range(1, n_sub):
+                all_sub[c, k, 0].wait_recv()
         total = sub_out[c, me_sub, me_slc, places[i]]
         for j in range(n_sub - 1):
             total = total + sub_in[c, j, me_slc, places[i]]
@@ -299,7 +306,8 @@
     for c in range(ahead, chunks):
         stem(c)
         send_sub(c)
-    for c in range(chunks):
+        to_slc(0, c - ahead)
+    for c in range(chunks - ahead, chunks):
         to_slc(0, c)
 
     if n_wide > 2:
@@ -365,7 +373,7 @@
         sin = out_sin[w * loc_pad:w * loc_pad + loc]
         out_ref[0, w] = real * cos + imag * sin
         out_ref[1, w] = imag * cos - real * sin
-    for copy in all_sub + list(all_slc.values()) + list(all_wide.values()):
+    for copy in list(all_sub.values()) + list(all_slc.values()) + list(all_wide.values()):
         copy.wait_send()
 
 
@@ -400,7 +408,7 @@
             pltpu.VMEM((chunks, 2, slices, bond, width), bf16),
             pltpu.VMEM((group, rows_loc, 128), f32),
             pltpu.VMEM((group, rows_loc, 128), f32),
-            pltpu.VMEM((tall, rows_loc), bf16),
+            pltpu.VMEM((tall, 2 * rows_loc), bf16),
             pltpu.VMEM((columns, columns), bf16),
             pltpu.VMEM((tall, columns), f32),
             pltpu.VMEM((tall, columns), f32),
@@ -414,8 +422,8 @@
             dma,
             dma,
             dma((chunks,)),
-            dma((chunks, n_sub - 1)),
-            dma((chunks, n_sub - 1)),
+            dma((chunks, n_sub - 1, n_slc)),
+            dma((chunks, n_sub - 1, n_slc)),
             dma((n_wide, chunks, n_slc - 1)),
             dma((n_wide, chunks, n_slc - 1)),
             dma((n_wide, chunks)),

time: 25 us -> 24.1 us (0.964)
  Pallas kernels: 23.3 us -> 22.3 us
    pallas_call x1, Pallas kernels: 23.3 us -> 22.3 us  [per_device(): pl.pallas_call(functools.partial(kernel_body, dims), out_shape=jax.ShapeD...]
where the time goes in v4:
time: 24.1 us; the launch traced here: 23.9 us
  Pallas kernels  22.3 us (93%)
  local copies, waits for them, and re-layouts  0.8 us (3%)
  other arithmetic  0.75 us (3%)
    pallas_call x1, Pallas kernels, per_device(): pl.pallas_call(functools.partial(kernel_body, dims), out_shape=jax.ShapeD...  22.3 us
    unnamed x1, local copies, waits for them, and re-layouts  0.8 us
    concatenate x1, other arithmetic, per_device(): choices = jnp.concatenate((gate_pick, leg_order))  0.75 us

profile of v4, /device:TPU:0, one launch (start us, length us, event | category | flops | bytes accessed | tf_op | source)
XLA Modules:
  0.0 23.9 jit_solution(8134223665825804445)
XLA Ops:
  0.0 0.7 %pad_add_fusion.pick_hbm = s32[29]{0:T(128)S(1)} fusion(s32[9]{0:T(128)} %param.7, s32[20]{0:T(128)} %param.6), kind=kLoop, calls=%fused_computation | loop fusion | flops 29 | bytes 232 | tf_op jit(solution)/shard_map/concatenate | solution.py:399
  0.7 22.3 %shard_map.46 = f32[2,4,32,512]{3,2,1,0:T(8,128)S(1)} custom-call(s32[29]{0:T(128)S(1)} %pad_add_fusion.pick_hbm, bf16[2,2,512,256]{3,2,1,0:T(8,128)(2,1)} %a_hbm.1, bf16[2,2,256,512]{3,2,1,0:T(8,128)(2,1)} %b_hbm.1), custom_call_target="tpu_custom_call" | custom-call | tf_op jit(solution)/shard_map/pallas_call | solution.py:400
  23.1 0.8 %copy.7 = f32[2,4,1,1,32,512]{5,4,3,2,1,0:T(8,128)} copy(f32[2,4,1,1,32,512]{5,4,3,2,1,0:T(8,128)S(1)} %bitcast.3) | data formatting | bytes 1048576
